TPU v7x, 32 devices: a whole 2x2x4 slice. The times are simulated.
32 devices in a mesh: animal: 8 (over z, y), snp: 4 (over x, core).
Axes of the slice: x: 2, y: 2, z: 4, core: 2. Of those that a mesh axis runs over, the one named last changes fastest.
Arguments:
- genotype: bfloat16 [8192, 32768], P('animal', 'snp')
- allele_freq: float32 [32768], P('snp')
- right_side: float32 [8192, 128], P('animal'), may hold values from -6 to 6
- diagonal: float32 [8192, 128], P('animal'), may hold values from 0.5 to 2
- mendelian: float32 [8192], P('animal'), may hold values from 2 to 4
- genomic_weight: float32 [128], replicated, may hold values from 1 to 8
- send_rows: int32 [8, 8, 64], P('animal'), may hold values from 0 to 1023, as said below
- sire_slot: int32 [8192], P('animal'), may hold values from 0 to 463, as said below
- dam_slot: int32 [8192], P('animal'), may hold values from 16 to 511, as said below
Outputs:
- solution: float32 [8192, 128], P('animal')
- residual: float32 [8192, 128], P('animal')
Inputs may be any that keep to these rules, and one draw needn't show every extreme that they name: send_rows[o, d, :] lists 64 distinct local rows of owner o's 1024 animals, those sent to device d. sire_slot[i] = o * 64 + k with k < 16. dam_slot[i] = o * 64 + k with k >= 16.
All inputs are finite; a program needn't handle non-finite values.
Results may differ from a plain program's by a relative error of at most 0.0067.
Values may be sent and summed in bfloat16 or wider, within the bound.
No kernel may reach another device: no remote copies, remote signals or barrier semaphores. Data moves between devices by JAX's collectives and lax.ppermute only.
A program may use at most 64 MiB of HBM per device.

v0:
```python
import jax
import jax.numpy as jnp
from jax import lax
from jax.sharding import PartitionSpec as P

SNPS = 32768
ITERS = 2


def local(
    genotype,
    allele_freq,
    right_side,
    diagonal,
    mendelian,
    genomic_weight,
    send_rows,
    sire_slot,
    dam_slot,
):
    owners = lax.axis_size("animal")
    slots = send_rows.shape[2]
    centered = (genotype.astype(jnp.float32) - 2.0 * allele_freq[None, :]).astype(jnp.bfloat16)
    outgoing_rows = send_rows[0]
    flat_rows = outgoing_rows.reshape(-1)
    scale = genomic_weight[None, :] / SNPS

    def pedigree(field):
        width = field.shape[1]
        outgoing = field[outgoing_rows]
        incoming = lax.all_to_all(outgoing, "animal", split_axis=0, concat_axis=0, tiled=True)
        received = incoming.reshape(owners * slots, width)
        mendel_term = mendelian[:, None] * (
            field - 0.5 * (received[sire_slot] + received[dam_slot])
        )
        back = jnp.zeros((owners * slots, width), jnp.float32)
        back = back.at[sire_slot].add(-0.5 * mendel_term).at[dam_slot].add(-0.5 * mendel_term)
        returned = lax.all_to_all(
            back.reshape(owners, slots, width), "animal", split_axis=0, concat_axis=0, tiled=True
        )
        return mendel_term + jnp.zeros_like(field).at[flat_rows].add(returned.reshape(-1, width))

    def genomic(field):
        field_b = field.astype(jnp.bfloat16)
        block = centered
        owned = lax.psum_scatter(
            lax.dot_general(
                block, field_b, (((0,), (0,)), ((), ())), preferred_element_type=jnp.float32
            ),
            "animal",
            scatter_dimension=0,
            tiled=True,
        )
        owned_b = owned.astype(jnp.bfloat16)
        block = centered
        partial_value = jnp.dot(
            block,
            lax.all_gather(owned_b, "animal", axis=0, tiled=True),
            preferred_element_type=jnp.float32,
        )
        return lax.psum(partial_value, "snp")

    def operate(field):
        ped = pedigree(field)
        return diagonal * field + ped + scale * genomic(field)

    solution = jnp.zeros_like(right_side)
    residual = right_side
    w_field = operate(residual)
    z_field = jnp.zeros_like(right_side)
    s_field = jnp.zeros_like(right_side)
    p_field = jnp.zeros_like(right_side)
    gamma_prev = None
    alpha_prev = None
    for step in range(ITERS):
        gamma, delta = lax.psum(
            (jnp.sum(residual * residual, axis=0), jnp.sum(w_field * residual, axis=0)), "animal"
        )
        q_field = operate(w_field)
        if step == 0:
            beta = jnp.zeros_like(gamma)
            alpha = gamma / delta
        else:
            beta = gamma / gamma_prev
            alpha = gamma / (delta - beta * gamma / alpha_prev)
        z_field = q_field + beta * z_field
        s_field = w_field + beta * s_field
        p_field = residual + beta * p_field
        solution = solution + alpha * p_field
        residual = residual - alpha * s_field
        w_field = w_field - alpha * z_field
        gamma_prev = gamma
        alpha_prev = alpha
    return (solution, residual)


def solution(mesh):
    placed = (
        P("animal", "snp"),
        P("snp"),
        P("animal", None),
        P("animal", None),
        P("animal"),
        P(),
        P("animal", None, None),
        P("animal"),
        P("animal"),
    )
    return jax.shard_map(
        local,
        mesh=mesh,
        in_specs=placed,
        out_specs=(P("animal", None), P("animal", None)),
        check_vma=False,
    )
```

profile of v0, /device:TPU:0, one launch (start us, length us, event | category | flops | bytes accessed | tf_op | source)
XLA Modules:
  0.0 508.4 jit_solution(10293679810259572106)
XLA Ops:
  7.2 0.0 reduce-scatter.3.cloned.1.call-start
  7.2 0.8 broadcast_multiply_fusion
  8.0 12.8 %fusion.3 = f32[8192,128]{1,0:T(8,128)} fusion(bf16[1024,8192]{1,0:T(8,128)(2,1)} %param.9, f32[8192]{0:T(1024)S(1)} %broadcast_multiply_fusion, f32[1024,128]{1,0:T(8,128)} %param.11), kind=kOutput, calls=%fused_computation.16 | convolution fusion | flops 2172780544 | bytes 21528576 | tf_op jit(solution)/shard_map/dot_general | solution.py:47
  20.8 0.0 reduce-scatter.3.cloned.1.call-update
  20.9 0.0 all-gather.3.cloned.1.call-start
  20.9 91.2 %reduce-scatter.3.cloned.1.call-done = f32[1024,128]{1,0:T(8,128)} async-done(((f32[8192,128]{1,0:T(8,128)}), f32[1024,128]{1,0:T(8,128)}) %reduce-scatter.3.cloned.1.call-update) | async-done | bytes 524304 | tf_op jit(solution)/shard_map/reduce_scatter | solution.py:46
  112.1 1.8 convert_element_type.21
  113.8 0.0 all-gather.3.cloned.1.call-update
  113.9 0.0 copy-done.2
  113.9 0.1 reshape.94
  114.0 0.0 copy-done
  114.0 1.6 gather_fusion
  115.6 4.2 all-to-all-start
  119.8 0.2 all-reduce.5.cloned.1.call-start
  120.1 0.0 copy-done.4
  120.1 0.0 copy-start.6
  120.1 0.0 copy-start.5
  120.1 0.0 copy-start.1
  120.1 0.0 copy-start.3
  120.1 45.6 %all-gather.3.cloned.1.call-done = bf16[8192,128]{1,0:T(8,128)(2,1)} async-done(((bf16[1024,128]{1,0:T(8,128)(2,1)}), bf16[8192,128]{1,0:T(8,128)(2,1)}) %all-gather.3.cloned.1.call-update) | async-done | bytes 2097168 | tf_op jit(solution)/shard_map/all_gather | solution.py:58
  165.7 11.7 %fusion.2 = f32[1024,128]{1,0:T(8,128)} fusion(bf16[8192,128]{1,0:T(8,128)(2,1)} %all-gather.3.cloned.1.call-done, bf16[1024,8192]{1,0:T(8,128)(2,1)} %param.9, f32[8192]{0:T(1024)S(1)} %broadcast_multiply_fusion), kind=kOutput, calls=%fused_computation.15 | convolution fusion | flops 2172649472 | bytes 19431424 | tf_op jit(solution)/shard_map/dot_general | solution.py:56
  177.4 0.0 all-reduce.5.cloned.1.call-update
  177.4 0.0 copy-done.6
  177.4 0.0 copy-done.5
  177.5 0.0 all-to-all-done
  177.5 2.8 gather_fusion.1
  180.3 2.8 gather_fusion.2
  183.1 26.3 %all-reduce.5.cloned.1.call-done = f32[1024,128]{1,0:T(8,128)} async-done(((f32[1024,128]{1,0:T(8,128)}), f32[1024,128]{1,0:T(8,128)}) %all-reduce.5.cloned.1.call-update) | async-done | bytes 524304 | tf_op jit(solution)/shard_map/psum | solution.py:61
  209.5 0.0 copy-done.1
  209.5 0.0 copy-done.3
  209.5 1.2 multiply_add_fusion.2
  210.7 6.7 %scatter_custom_fusion = f32[512,128]{1,0:T(8,128)} fusion(s32[1024]{0:T(1024)S(1)} %get-tuple-element.22, f32[1024,128]{1,0:T(8,128)S(1)} %get-tuple-element.15, f32[]{:T(128)} %constant.3.clone.1, f32[]{:T(128)} %constant.8.clone.1), kind=kCustom, calls=%fused_computation.35 | custom fusion | flops 262144 | bytes 786440 | tf_op jit(solution)/shard_map/scatter-add | solution.py:37
  217.4 7.1 %scatter_custom_fusion.1 = f32[512,128]{1,0:T(8,128)} fusion(f32[512,128]{1,0:T(8,128)} %scatter_custom_fusion, s32[1024]{0:T(1024)S(1)} %get-tuple-element.20, f32[1024,128]{1,0:T(8,128)S(1)} %get-tuple-element.15, f32[]{:T(128)} %constant.3.clone.1), kind=kCustom, calls=%fused_computation.33 | custom fusion | flops 262144 | bytes 786944 | tf_op jit(solution)/shard_map/scatter-add | solution.py:37
  224.6 5.5 %all-to-all-start.1 = ((f32[8,64,128]{2,1,0:T(8,128)}), f32[8,64,128]{2,1,0:T(8,128)S(1)}, u32[]{:S(2)}, u32[]{:S(2)}) async-start(f32[8,64,128]{2,1,0:T(8,128)} %bitcast.4), calls=%async_computation.2 | async-start | bytes 524288 | tf_op jit(solution)/shard_map/all_to_all | solution.py:38
  230.1 0.0 reduce-scatter.5.cloned.1.call-start
  230.1 0.1 reshape_squeeze.3
  230.2 8.1 %all-to-all-done.1 = f32[8,64,128]{2,1,0:T(8,128)S(1)} async-done(((f32[8,64,128]{2,1,0:T(8,128)}), f32[8,64,128]{2,1,0:T(8,128)S(1)}, u32[]{:S(2)}, u32[]{:S(2)}) %all-to-all-start.1) | async-done | bytes 262176 | tf_op jit(solution)/shard_map/all_to_all | solution.py:38
  238.3 3.7 scatter_fusion
  242.0 10.5 %fusion.1 = f32[8192,128]{1,0:T(8,128)} fusion(bf16[1024,8192]{1,0:T(8,128)(2,1)} %param.9, f32[8192]{0:T(1024)S(1)} %broadcast_multiply_fusion, f32[1024,128]{1,0:T(8,128)S(1)} %scatter_fusion), kind=kOutput, calls=%fused_computation.14 | convolution fusion | flops 2172780544 | bytes 21528576 | tf_op jit(solution)/shard_map/dot_general | solution.py:47
  252.5 0.0 reduce-scatter.5.cloned.1.call-update
  252.5 0.0 all-gather.5.cloned.1.call-start
  252.6 86.7 %reduce-scatter.5.cloned.1.call-done = f32[1024,128]{1,0:T(8,128)} async-done(((f32[8192,128]{1,0:T(8,128)}), f32[1024,128]{1,0:T(8,128)}) %reduce-scatter.5.cloned.1.call-update) | async-done | bytes 524304 | tf_op jit(solution)/shard_map/reduce_scatter | solution.py:46
  339.3 1.8 convert_element_type.23
  341.0 0.0 all-gather.5.cloned.1.call-update
  341.1 1.6 gather_fusion.3
  342.7 4.2 all-to-all-start.2
  347.0 0.0 all-reduce.7.cloned.1.call-start
  347.0 45.8 %all-gather.5.cloned.1.call-done = bf16[8192,128]{1,0:T(8,128)(2,1)} async-done(((bf16[1024,128]{1,0:T(8,128)(2,1)}), bf16[8192,128]{1,0:T(8,128)(2,1)}) %all-gather.5.cloned.1.call-update) | async-done | bytes 2097168 | tf_op jit(solution)/shard_map/all_gather | solution.py:58
  392.8 11.7 %fusion = f32[1024,128]{1,0:T(8,128)} fusion(bf16[8192,128]{1,0:T(8,128)(2,1)} %all-gather.5.cloned.1.call-done, bf16[1024,8192]{1,0:T(8,128)(2,1)} %param.9, f32[8192]{0:T(1024)S(1)} %broadcast_multiply_fusion), kind=kOutput, calls=%fused_computation.13 | convolution fusion | flops 2172649472 | bytes 19431424 | tf_op jit(solution)/shard_map/dot_general | solution.py:56
  404.5 0.0 all-reduce.7.cloned.1.call-update
  404.5 0.0 all-to-all-done.2
  404.5 2.8 gather_fusion.4
  407.3 4.0 gather_fusion.5
  411.4 25.2 %all-reduce.7.cloned.1.call-done = f32[1024,128]{1,0:T(8,128)} async-done(((f32[1024,128]{1,0:T(8,128)}), f32[1024,128]{1,0:T(8,128)}) %all-reduce.7.cloned.1.call-update) | async-done | bytes 524304 | tf_op jit(solution)/shard_map/psum | solution.py:61
  436.6 1.5 multiply_reduce_fusion.2
  438.1 6.7 %scatter_custom_fusion.3 = f32[512,128]{1,0:T(8,128)} fusion(s32[1024]{0:T(1024)S(1)} %get-tuple-element.22, f32[1024,128]{1,0:T(8,128)S(1)} %get-tuple-element.19, f32[]{:T(128)} %constant.3.clone.1, f32[]{:T(128)} %constant.8.clone.1), kind=kCustom, calls=%fused_computation.31 | custom fusion | flops 262144 | bytes 786440 | tf_op jit(solution)/shard_map/scatter-add | solution.py:37
  444.8 7.1 %scatter_custom_fusion.4 = f32[512,128]{1,0:T(8,128)} fusion(f32[512,128]{1,0:T(8,128)} %scatter_custom_fusion.3, s32[1024]{0:T(1024)S(1)} %get-tuple-element.20, f32[1024,128]{1,0:T(8,128)S(1)} %get-tuple-element.19, f32[]{:T(128)} %constant.3.clone.1), kind=kCustom, calls=%fused_computation.29 | custom fusion | flops 262144 | bytes 786944 | tf_op jit(solution)/shard_map/scatter-add | solution.py:37
  451.9 5.5 %all-to-all-start.3 = ((f32[8,64,128]{2,1,0:T(8,128)}), f32[8,64,128]{2,1,0:T(8,128)S(1)}, u32[]{:S(2)}, u32[]{:S(2)}) async-start(f32[8,64,128]{2,1,0:T(8,128)} %bitcast.8), calls=%async_computation.5 | async-start | bytes 524288 | tf_op jit(solution)/shard_map/all_to_all | solution.py:38
  457.4 21.8 %all-reduce.1 = (f32[128]{0:T(128)S(1)}, f32[128]{0:T(128)S(1)}) all-reduce(f32[128]{0:T(128)S(1)} %get-tuple-element.5, f32[128]{0:T(128)S(1)} %get-tuple-element.4), channel_id=1, replica_groups=mesh['animal'=8,'snp'=4] {'animal'}, use_global_device_ids=true, to_apply=%region_1.0 | all-reduce | flops 256 | bytes 2048 | tf_op jit(solution)/shard_map/psum | solution.py:76
  479.2 0.0 all-to-all-done.3
  479.2 3.8 scatter_fusion.1
  483.0 0.2 multiply_reduce_fusion
  483.2 17.1 %all-reduce = (f32[128]{0:T(128)S(1)}, f32[128]{0:T(128)S(1)}) all-reduce(f32[128]{0:T(128)S(1)} %get-tuple-element.3, f32[128]{0:T(128)S(1)} %get-tuple-element.2), channel_id=1, replica_groups=mesh['animal'=8,'snp'=4] {'animal'}, use_global_device_ids=true, to_apply=%region_10.0 | all-reduce | flops 256 | bytes 2048 | tf_op jit(solution)/shard_map/psum | solution.py:76
  500.3 1.2 multiply_subtract_fusion
  (11 shorter events, 0.1 us)
Async XLA Ops:
  7.2 104.9 %reduce-scatter.3.cloned.1.call-start = ((), (), s32[]{:S(2)}) async-start(), calls=%async_computation.6 | async-start | bytes 4718592 | tf_op jit(solution)/shard_map/reduce_scatter | solution.py:46
  8.0 105.9 %copy-start.2 = (s32[1,8,64]{2,1,0:T(8,128)S(1)}, s32[1,8,64]{2,1,0:T(8,128)}, u32[]{:S(2)}) copy-start(s32[1,8,64]{2,1,0:T(8,128)} %param.15) | copy-start | bytes 6148
  8.0 106.0 %copy-start = (f32[1024,128]{1,0:T(8,128)S(1)}, f32[1024,128]{1,0:T(8,128)}, u32[]{:S(2)}) copy-start(f32[1024,128]{1,0:T(8,128)} %param.11) | copy-start | bytes 1572868
  8.0 112.1 %copy-start.4 = (s32[1024]{0:T(1024)S(1)}, s32[1024]{0:T(1024)}, u32[]{:S(2)}) copy-start(s32[1024]{0:T(1024)} %param.16) | copy-start | bytes 12292
  20.9 144.9 %all-gather.3.cloned.1.call-start = ((), (), s32[]{:S(2)}) async-start(), calls=%async_computation.7 | async-start | bytes 2359296 | tf_op jit(solution)/shard_map/all_gather | solution.py:58
  115.6 61.9 %all-to-all-start = ((f32[8,64,128]{2,1,0:T(8,128)}), f32[8,64,128]{2,1,0:T(8,128)S(1)}, u32[]{:S(2)}, u32[]{:S(2)}) async-start(f32[8,64,128]{2,1,0:T(8,128)} %bitcast.1), calls=%async_computation | async-start | bytes 524288 | tf_op jit(solution)/shard_map/all_to_all | solution.py:31
  119.8 89.6 %all-reduce.5.cloned.1.call-start = ((), (), s32[]{:S(2)}) async-start(), calls=%async_computation.8 | async-start | bytes 1048576 | tf_op jit(solution)/shard_map/psum | solution.py:61
  120.1 57.3 %copy-start.6 = (f32[128]{0:T(128)S(1)}, f32[128]{0:T(128)}, u32[]{:S(2)}) copy-start(f32[128]{0:T(128)} %param.14) | copy-start | bytes 1540
  120.1 57.3 %copy-start.5 = (s32[1024]{0:T(1024)S(1)}, s32[1024]{0:T(1024)}, u32[]{:S(2)}) copy-start(s32[1024]{0:T(1024)} %param.17) | copy-start | bytes 12292
  120.1 89.3 %copy-start.1 = (f32[1024,128]{1,0:T(8,128)S(1)}, f32[1024,128]{1,0:T(8,128)}, u32[]{:S(2)}) copy-start(f32[1024,128]{1,0:T(8,128)} %param.12) | copy-start | bytes 1572868
  120.1 89.3 %copy-start.3 = (f32[1024]{0:T(1024)S(1)}, f32[1024]{0:T(1024)}, u32[]{:S(2)}) copy-start(f32[1024]{0:T(1024)} %param.13) | copy-start | bytes 12292
  224.6 13.7 %all-to-all-start.1 = ((f32[8,64,128]{2,1,0:T(8,128)}), f32[8,64,128]{2,1,0:T(8,128)S(1)}, u32[]{:S(2)}, u32[]{:S(2)}) async-start(f32[8,64,128]{2,1,0:T(8,128)} %bitcast.4), calls=%async_computation.2 | async-start | bytes 524288 | tf_op jit(solution)/shard_map/all_to_all | solution.py:38
  230.1 109.2 %reduce-scatter.5.cloned.1.call-start = ((), (), s32[]{:S(2)}) async-start(), calls=%async_computation.9 | async-start | bytes 4718592 | tf_op jit(solution)/shard_map/reduce_scatter | solution.py:46
  252.5 140.3 %all-gather.5.cloned.1.call-start = ((), (), s32[]{:S(2)}) async-start(), calls=%async_computation.10 | async-start | bytes 2359296 | tf_op jit(solution)/shard_map/all_gather | solution.py:58
  342.7 61.8 %all-to-all-start.2 = ((f32[8,64,128]{2,1,0:T(8,128)}), f32[8,64,128]{2,1,0:T(8,128)S(1)}, u32[]{:S(2)}, u32[]{:S(2)}) async-start(f32[8,64,128]{2,1,0:T(8,128)} %bitcast.6), calls=%async_computation.3 | async-start | bytes 524288 | tf_op jit(solution)/shard_map/all_to_all | solution.py:31
  347.0 89.7 %all-reduce.7.cloned.1.call-start = ((), (), s32[]{:S(2)}) async-start(), calls=%async_computation.11 | async-start | bytes 1048576 | tf_op jit(solution)/shard_map/psum | solution.py:61
  451.9 27.3 %all-to-all-start.3 = ((f32[8,64,128]{2,1,0:T(8,128)}), f32[8,64,128]{2,1,0:T(8,128)S(1)}, u32[]{:S(2)}, u32[]{:S(2)}) async-start(f32[8,64,128]{2,1,0:T(8,128)} %bitcast.8), calls=%async_computation.5 | async-start | bytes 524288 | tf_op jit(solution)/shard_map/all_to_all | solution.py:38
Sparse Core Ops, SparseCore 0:
  21.0 91.0 reduce-scatter.2
  114.8 50.9 all-gather.2
  177.5 31.8 all-reduce.4
  252.6 86.5 reduce-scatter.4
  341.8 50.9 all-gather.4
  404.6 31.9 all-reduce.6
where the time goes:
time: 509 us; the launch traced here: 508 us
  waiting for transfers between devices  329 us (65%)
  matrix products  46.6 us (9%)
  other arithmetic  43.6 us (9%)
  blocking collectives  39 us (8%)
  starting transfers between devices  19.9 us (4%)
  local copies, waits for them, and re-layouts  16 us (3%)
  between operations  14.3 us (3%)
    reduce_scatter x2, waiting for transfers between devices, genomic(): lax.psum_scatter(lax.dot_general(block, field_b, (((0,), (0,)), ((), ()))...  178 us
    all_gather x2, waiting for transfers between devices, genomic(): lax.all_gather(owned_b, 'animal', axis=0, tiled=True)  91.4 us
    psum x2, waiting for transfers between devices, genomic(): return lax.psum(partial_value, 'snp')  51.6 us
    psum x2, blocking collectives, local(): lax.psum((jnp.sum(residual * residual, axis=0), jnp.sum(w_field * residua...  39 us
    scatter-add x4, other arithmetic, pedigree(): back.at[sire_slot].add(-0.5 * mendel_term).at[dam_slot]  27.7 us
    dot_general x2, matrix products, genomic(): jnp.dot(block, lax.all_gather(owned_b, 'animal', axis=0, tiled=True), pre...  23.3 us
    dot_general x2, matrix products, genomic(): lax.dot_general(block, field_b, (((0,), (0,)), ((), ())), preferred_eleme...  23.3 us
    all_to_all x2, starting transfers between devices, pedigree(): lax.all_to_all(back.reshape(owners, slots, width), 'animal', split_axis=0...  11 us
  transfers between devices with their start and end apart: 10, of which 7 were waited for; matrix products, arithmetic and copies ran while one was open for 8% of the time, Pallas kernels for 0%

commit v1 on v0

--- a/solution.py
+++ b/solution.py
@@ -58,7 +58,7 @@
             lax.all_gather(owned_b, "animal", axis=0, tiled=True),
             preferred_element_type=jnp.float32,
         )
-        return lax.psum(partial_value, "snp")
+        return jnp.sum(lax.all_gather(partial_value, "snp"), axis=0)
 
     def operate(field):
         ped = pedigree(field)

time: 509 us -> 487 us (0.957)
  waiting for transfers between devices: 329 us -> 295 us
  blocking collectives: 39 us -> 50.4 us
    psum x2 -> x0, waiting for transfers between devices: 51.6 us -> none  [genomic(): return lax.psum(partial_value, 'snp')]
    all_to_all x0 -> x1, blocking collectives: none -> 11.4 us  [pedigree(): lax.all_to_all(outgoing, 'animal', split_axis=0, concat_axis=0, tiled=True)]
    all_to_all x2 -> x1, waiting for transfers between devices: 0.01 us -> 7.93 us  [pedigree(): lax.all_to_all(outgoing, 'animal', split_axis=0, concat_axis=0, tiled=True)]
    all_gather x2, waiting for transfers between devices: 91.4 us -> 98.8 us  [genomic(): lax.all_gather(owned_b, 'animal', axis=0, tiled=True)]
  transfers between devices with their start and end apart: 10 -> 9, of which waited for: 7 -> 8; matrix products, arithmetic and copies ran while one was open for 8% -> 4% of each run, Pallas kernels for 0% -> 0%
where the time goes in v1:
time: 487 us; the launch traced here: 486 us
  waiting for transfers between devices  295 us (61%)
  blocking collectives  50.4 us (10%)
  other arithmetic  46.6 us (10%)
  matrix products  46.6 us (10%)
  local copies, waits for them, and re-layouts  17.7 us (4%)
  starting transfers between devices  15.1 us (3%)
  between operations  14.3 us (3%)
    reduce_scatter x2, waiting for transfers between devices, genomic(): lax.psum_scatter(lax.dot_general(block, field_b, (((0,), (0,)), ((), ()))...  178 us
    all_gather x2, waiting for transfers between devices, genomic(): lax.all_gather(owned_b, 'animal', axis=0, tiled=True)  98.8 us
    psum x2, blocking collectives, local(): lax.psum((jnp.sum(residual * residual, axis=0), jnp.sum(w_field * residua...  39 us
    scatter-add x4, other arithmetic, pedigree(): back.at[sire_slot].add(-0.5 * mendel_term).at[dam_slot]  27.7 us
    dot_general x2, matrix products, genomic(): jnp.dot(block, lax.all_gather(owned_b, 'animal', axis=0, tiled=True), pre...  23.3 us
    dot_general x2, matrix products, genomic(): lax.dot_general(block, field_b, (((0,), (0,)), ((), ())), preferred_eleme...  23.3 us
    all_to_all x1, blocking collectives, pedigree(): lax.all_to_all(outgoing, 'animal', split_axis=0, concat_axis=0, tiled=True)  11.4 us
    all_to_all x2, starting transfers between devices, pedigree(): lax.all_to_all(back.reshape(owners, slots, width), 'animal', split_axis=0...  11 us
  transfers between devices with their start and end apart: 9, of which 8 were waited for; matrix products, arithmetic and copies ran while one was open for 4% of the time, Pallas kernels for 0%

profile of v1, /device:TPU:0, one launch (start us, length us, event | category | flops | bytes accessed | tf_op | source)
XLA Modules:
  0.0 486.2 jit_solution(1548471708739226769)
XLA Ops:
  7.2 0.0 reduce-scatter.3.cloned.1.call-start
  7.2 0.8 broadcast_multiply_fusion
  8.0 12.8 %fusion.3 = f32[8192,128]{1,0:T(8,128)} fusion(bf16[1024,8192]{1,0:T(8,128)(2,1)} %param.9, f32[8192]{0:T(1024)S(1)} %broadcast_multiply_fusion, f32[1024,128]{1,0:T(8,128)} %param.11), kind=kOutput, calls=%fused_computation.16 | convolution fusion | flops 2172780544 | bytes 21528576 | tf_op jit(solution)/shard_map/dot_general | solution.py:47
  20.8 0.0 reduce-scatter.3.cloned.1.call-update
  20.8 0.0 all-gather.7.cloned.1.call-start
  20.8 91.2 %reduce-scatter.3.cloned.1.call-done = f32[1024,128]{1,0:T(8,128)} async-done(((f32[8192,128]{1,0:T(8,128)}), f32[1024,128]{1,0:T(8,128)}) %reduce-scatter.3.cloned.1.call-update) | async-done | bytes 524304 | tf_op jit(solution)/shard_map/reduce_scatter | solution.py:46
  112.0 1.8 convert_element_type.21
  113.8 0.0 all-gather.7.cloned.1.call-update
  113.8 0.0 copy-start.2
  113.8 0.0 copy-start
  113.8 0.0 copy-start.6
  113.8 0.0 copy-start.4
  113.8 0.0 copy-start.5
  113.8 0.0 copy-start.1
  113.9 0.0 copy-start.3
  113.9 0.0 all-gather.11.cloned.1.call-start
  113.9 49.5 %all-gather.7.cloned.1.call-done = bf16[8192,128]{1,0:T(8,128)(2,1)} async-done(((bf16[1024,128]{1,0:T(8,128)(2,1)}), bf16[8192,128]{1,0:T(8,128)(2,1)}) %all-gather.7.cloned.1.call-update) | async-done | bytes 2097168 | tf_op jit(solution)/shard_map/all_gather | solution.py:58
  163.5 11.7 %fusion.2 = f32[1024,128]{1,0:T(8,128)} fusion(bf16[8192,128]{1,0:T(8,128)(2,1)} %all-gather.7.cloned.1.call-done, bf16[1024,8192]{1,0:T(8,128)(2,1)} %param.9, f32[8192]{0:T(1024)S(1)} %broadcast_multiply_fusion), kind=kOutput, calls=%fused_computation.15 | convolution fusion | flops 2172649472 | bytes 19431424 | tf_op jit(solution)/shard_map/dot_general | solution.py:56
  175.1 0.0 all-gather.11.cloned.1.call-update
  175.2 0.0 copy-done.2
  175.2 0.1 reshape.94
  175.3 0.0 copy-done
  175.3 1.6 gather_fusion
  176.9 3.6 all-to-all-start
  180.6 0.0 copy-done.5
  180.6 7.9 %all-to-all-done = f32[8,64,128]{2,1,0:T(8,128)S(1)} async-done(((f32[8,64,128]{2,1,0:T(8,128)}), f32[8,64,128]{2,1,0:T(8,128)S(1)}, u32[]{:S(2)}, u32[]{:S(2)}) %all-to-all-start) | async-done | bytes 262176 | tf_op jit(solution)/shard_map/all_to_all | solution.py:31
  188.5 2.8 gather_fusion.1
  191.3 4.0 gather_fusion.2
  195.4 1.0 all-gather.11.cloned.1.call-done
  196.4 1.8 reduce_sum.55
  198.2 1.2 multiply_add_fusion.2
  199.4 6.7 %scatter_custom_fusion = f32[512,128]{1,0:T(8,128)} fusion(s32[1024]{0:T(1024)S(1)} %get-tuple-element.22, f32[1024,128]{1,0:T(8,128)S(1)} %get-tuple-element.15, f32[]{:T(128)} %constant.3.clone.1, f32[]{:T(128)} %constant.8.clone.1), kind=kCustom, calls=%fused_computation.35 | custom fusion | flops 262144 | bytes 786440 | tf_op jit(solution)/shard_map/scatter-add | solution.py:37
  206.2 7.1 %scatter_custom_fusion.1 = f32[512,128]{1,0:T(8,128)} fusion(f32[512,128]{1,0:T(8,128)} %scatter_custom_fusion, s32[1024]{0:T(1024)S(1)} %get-tuple-element.20, f32[1024,128]{1,0:T(8,128)S(1)} %get-tuple-element.15, f32[]{:T(128)} %constant.3.clone.1), kind=kCustom, calls=%fused_computation.33 | custom fusion | flops 262144 | bytes 786944 | tf_op jit(solution)/shard_map/scatter-add | solution.py:37
  213.3 5.5 %all-to-all-start.1 = ((f32[8,64,128]{2,1,0:T(8,128)}), f32[8,64,128]{2,1,0:T(8,128)S(1)}, u32[]{:S(2)}, u32[]{:S(2)}) async-start(f32[8,64,128]{2,1,0:T(8,128)} %bitcast.5), calls=%async_computation.2 | async-start | bytes 524288 | tf_op jit(solution)/shard_map/all_to_all | solution.py:38
  218.8 0.0 reduce-scatter.5.cloned.1.call-start
  218.8 0.1 reshape_squeeze.3
  218.9 9.2 %all-to-all-done.1 = f32[8,64,128]{2,1,0:T(8,128)S(1)} async-done(((f32[8,64,128]{2,1,0:T(8,128)}), f32[8,64,128]{2,1,0:T(8,128)S(1)}, u32[]{:S(2)}, u32[]{:S(2)}) %all-to-all-start.1) | async-done | bytes 262176 | tf_op jit(solution)/shard_map/all_to_all | solution.py:38
  228.1 3.5 scatter_fusion
  231.6 10.5 %fusion.1 = f32[8192,128]{1,0:T(8,128)} fusion(bf16[1024,8192]{1,0:T(8,128)(2,1)} %param.9, f32[8192]{0:T(1024)S(1)} %broadcast_multiply_fusion, f32[1024,128]{1,0:T(8,128)S(1)} %scatter_fusion), kind=kOutput, calls=%fused_computation.14 | convolution fusion | flops 2172780544 | bytes 21528576 | tf_op jit(solution)/shard_map/dot_general | solution.py:47
  242.1 0.0 reduce-scatter.5.cloned.1.call-update
  242.1 0.0 all-gather.9.cloned.1.call-start
  242.1 86.5 %reduce-scatter.5.cloned.1.call-done = f32[1024,128]{1,0:T(8,128)} async-done(((f32[8192,128]{1,0:T(8,128)}), f32[1024,128]{1,0:T(8,128)}) %reduce-scatter.5.cloned.1.call-update) | async-done | bytes 524304 | tf_op jit(solution)/shard_map/reduce_scatter | solution.py:46
  328.6 1.8 convert_element_type.23
  330.4 0.0 all-gather.9.cloned.1.call-update
  330.4 0.3 all-gather.13.cloned.1.call-start
  330.7 49.3 %all-gather.9.cloned.1.call-done = bf16[8192,128]{1,0:T(8,128)(2,1)} async-done(((bf16[1024,128]{1,0:T(8,128)(2,1)}), bf16[8192,128]{1,0:T(8,128)(2,1)}) %all-gather.9.cloned.1.call-update) | async-done | bytes 2097168 | tf_op jit(solution)/shard_map/all_gather | solution.py:58
  379.9 11.7 %fusion = f32[1024,128]{1,0:T(8,128)} fusion(bf16[8192,128]{1,0:T(8,128)(2,1)} %all-gather.9.cloned.1.call-done, bf16[1024,8192]{1,0:T(8,128)(2,1)} %param.9, f32[8192]{0:T(1024)S(1)} %broadcast_multiply_fusion), kind=kOutput, calls=%fused_computation.13 | convolution fusion | flops 2172649472 | bytes 19431424 | tf_op jit(solution)/shard_map/dot_general | solution.py:56
  391.6 0.0 all-gather.13.cloned.1.call-update
  391.6 1.0 gather_fusion.3
  392.7 11.4 %all_to_all.20 = f32[8,64,128]{2,1,0:T(8,128)S(1)} all-to-all(f32[8,64,128]{2,1,0:T(8,128)S(1)} %bitcast.25), channel_id=1, replica_groups=mesh['animal'=8,'snp'=4] {'animal'}, dimensions={0} | all-to-all | bytes 524288 | tf_op jit(solution)/shard_map/all_to_all | solution.py:31
  404.1 4.0 gather_fusion.4
  408.1 4.0 gather_fusion.5
  412.1 0.8 all-gather.13.cloned.1.call-done
  412.9 1.8 reduce_sum.58
  414.7 1.5 multiply_reduce_fusion.2
  416.1 6.7 %scatter_custom_fusion.3 = f32[512,128]{1,0:T(8,128)} fusion(s32[1024]{0:T(1024)S(1)} %get-tuple-element.22, f32[1024,128]{1,0:T(8,128)S(1)} %get-tuple-element.19, f32[]{:T(128)} %constant.3.clone.1, f32[]{:T(128)} %constant.8.clone.1), kind=kCustom, calls=%fused_computation.31 | custom fusion | flops 262144 | bytes 786440 | tf_op jit(solution)/shard_map/scatter-add | solution.py:37
  422.8 7.1 %scatter_custom_fusion.4 = f32[512,128]{1,0:T(8,128)} fusion(f32[512,128]{1,0:T(8,128)} %scatter_custom_fusion.3, s32[1024]{0:T(1024)S(1)} %get-tuple-element.20, f32[1024,128]{1,0:T(8,128)S(1)} %get-tuple-element.19, f32[]{:T(128)} %constant.3.clone.1), kind=kCustom, calls=%fused_computation.29 | custom fusion | flops 262144 | bytes 786944 | tf_op jit(solution)/shard_map/scatter-add | solution.py:37
  429.9 5.5 %all-to-all-start.3 = ((f32[8,64,128]{2,1,0:T(8,128)}), f32[8,64,128]{2,1,0:T(8,128)S(1)}, u32[]{:S(2)}, u32[]{:S(2)}) async-start(f32[8,64,128]{2,1,0:T(8,128)} %bitcast.10), calls=%async_computation.5 | async-start | bytes 524288 | tf_op jit(solution)/shard_map/all_to_all | solution.py:38
  435.5 21.8 %all-reduce.1 = (f32[128]{0:T(128)S(1)}, f32[128]{0:T(128)S(1)}) all-reduce(f32[128]{0:T(128)S(1)} %get-tuple-element.5, f32[128]{0:T(128)S(1)} %get-tuple-element.4), channel_id=1, replica_groups=mesh['animal'=8,'snp'=4] {'animal'}, use_global_device_ids=true, to_apply=%region_1.0 | all-reduce | flops 256 | bytes 2048 | tf_op jit(solution)/shard_map/psum | solution.py:76
  457.3 0.0 all-to-all-done.3
  457.3 3.5 scatter_fusion.1
  460.8 0.2 multiply_reduce_fusion
  461.0 17.1 %all-reduce = (f32[128]{0:T(128)S(1)}, f32[128]{0:T(128)S(1)}) all-reduce(f32[128]{0:T(128)S(1)} %get-tuple-element.3, f32[128]{0:T(128)S(1)} %get-tuple-element.2), channel_id=1, replica_groups=mesh['animal'=8,'snp'=4] {'animal'}, use_global_device_ids=true, to_apply=%region_10.0 | all-reduce | flops 256 | bytes 2048 | tf_op jit(solution)/shard_map/psum | solution.py:76
  478.1 1.2 multiply_subtract_fusion
  (12 shorter events, 0.1 us)
Async XLA Ops:
  7.2 104.8 %reduce-scatter.3.cloned.1.call-start = ((), (), s32[]{:S(2)}) async-start(), calls=%async_computation.6 | async-start | bytes 4718592 | tf_op jit(solution)/shard_map/reduce_scatter | solution.py:46
  20.8 142.7 %all-gather.7.cloned.1.call-start = ((), (), s32[]{:S(2)}) async-start(), calls=%async_computation.7 | async-start | bytes 2359296 | tf_op jit(solution)/shard_map/all_gather | solution.py:58
  113.8 61.4 %copy-start.2 = (s32[1,8,64]{2,1,0:T(8,128)S(1)}, s32[1,8,64]{2,1,0:T(8,128)}, u32[]{:S(2)}) copy-start(s32[1,8,64]{2,1,0:T(8,128)} %param.15) | copy-start | bytes 6148
  113.8 61.5 %copy-start = (f32[1024,128]{1,0:T(8,128)S(1)}, f32[1024,128]{1,0:T(8,128)}, u32[]{:S(2)}) copy-start(f32[1024,128]{1,0:T(8,128)} %param.11) | copy-start | bytes 1572868
  113.8 66.7 %copy-start.6 = (f32[128]{0:T(128)S(1)}, f32[128]{0:T(128)}, u32[]{:S(2)}) copy-start(f32[128]{0:T(128)} %param.14) | copy-start | bytes 1540
  113.8 66.7 %copy-start.4 = (s32[1024]{0:T(1024)S(1)}, s32[1024]{0:T(1024)}, u32[]{:S(2)}) copy-start(s32[1024]{0:T(1024)} %param.16) | copy-start | bytes 12292
  113.8 66.7 %copy-start.5 = (s32[1024]{0:T(1024)S(1)}, s32[1024]{0:T(1024)}, u32[]{:S(2)}) copy-start(s32[1024]{0:T(1024)} %param.17) | copy-start | bytes 12292
  113.8 84.3 %copy-start.1 = (f32[1024,128]{1,0:T(8,128)S(1)}, f32[1024,128]{1,0:T(8,128)}, u32[]{:S(2)}) copy-start(f32[1024,128]{1,0:T(8,128)} %param.12) | copy-start | bytes 1572868
  113.9 84.3 %copy-start.3 = (f32[1024]{0:T(1024)S(1)}, f32[1024]{0:T(1024)}, u32[]{:S(2)}) copy-start(f32[1024]{0:T(1024)} %param.13) | copy-start | bytes 12292
  113.9 82.5 %all-gather.11.cloned.1.call-start = ((), (), s32[]{:S(2)}) async-start(), calls=%async_computation.10 | async-start | bytes 2621440 | tf_op jit(solution)/shard_map/all_gather | solution.py:61
  176.9 11.6 %all-to-all-start = ((f32[8,64,128]{2,1,0:T(8,128)}), f32[8,64,128]{2,1,0:T(8,128)S(1)}, u32[]{:S(2)}, u32[]{:S(2)}) async-start(f32[8,64,128]{2,1,0:T(8,128)} %bitcast.1), calls=%async_computation | async-start | bytes 524288 | tf_op jit(solution)/shard_map/all_to_all | solution.py:31
  213.3 14.8 %all-to-all-start.1 = ((f32[8,64,128]{2,1,0:T(8,128)}), f32[8,64,128]{2,1,0:T(8,128)S(1)}, u32[]{:S(2)}, u32[]{:S(2)}) async-start(f32[8,64,128]{2,1,0:T(8,128)} %bitcast.5), calls=%async_computation.2 | async-start | bytes 524288 | tf_op jit(solution)/shard_map/all_to_all | solution.py:38
  218.8 109.8 %reduce-scatter.5.cloned.1.call-start = ((), (), s32[]{:S(2)}) async-start(), calls=%async_computation.8 | async-start | bytes 4718592 | tf_op jit(solution)/shard_map/reduce_scatter | solution.py:46
  242.1 137.9 %all-gather.9.cloned.1.call-start = ((), (), s32[]{:S(2)}) async-start(), calls=%async_computation.9 | async-start | bytes 2359296 | tf_op jit(solution)/shard_map/all_gather | solution.py:58
  330.4 82.5 %all-gather.13.cloned.1.call-start = ((), (), s32[]{:S(2)}) async-start(), calls=%async_computation.11 | async-start | bytes 2621440 | tf_op jit(solution)/shard_map/all_gather | solution.py:61
  429.9 27.3 %all-to-all-start.3 = ((f32[8,64,128]{2,1,0:T(8,128)}), f32[8,64,128]{2,1,0:T(8,128)S(1)}, u32[]{:S(2)}, u32[]{:S(2)}) async-start(f32[8,64,128]{2,1,0:T(8,128)} %bitcast.10), calls=%async_computation.5 | async-start | bytes 524288 | tf_op jit(solution)/shard_map/all_to_all | solution.py:38
Sparse Core Ops, SparseCore 0:
  20.9 91.0 reduce-scatter.2
  114.7 48.7 all-gather.6
  175.3 21.0 all-gather.10
  242.2 86.3 reduce-scatter.4
  331.2 48.7 all-gather.8
  391.8 21.0 all-gather.12
